TPU v7x, 32 devices: a whole 2x2x4 slice. The times are simulated.
32 devices in a mesh: col: 16 (over z, y, x), grp: 2 (over core).
Axes of the slice: x: 2, y: 2, z: 4, core: 2. Of those that a mesh axis runs over, the one named last changes fastest.
Arguments:
- diag_blocks: float32 [16, 128, 128], P('col'), as said below
- panel_blocks: float32 [16, 2, 128, 128], P('col', 'grp'), as said below
- targets: int32 [16, 2], replicated, may hold values from 0 to 16, as said below
Outputs:
- factor_diag: float32 [16, 128, 128], P('col')
- factor_panel: float32 [16, 2, 128, 128], P('col', 'grp')
Inputs may be any that keep to these rules, and one draw needn't show every extreme that they name: targets[s, 0] is the parent of supernode s and targets[s, 1] = targets[targets[s, 0], 0] its grandparent, 16 where that ancestor lies outside the window; the tree is a binary heap under a random labelling: exactly one root, every supernode has at most two children and at most four grandchildren, and level d holds min(2 ** d, 16 - 2 ** d + 1) supernodes. `diag_blocks`: each block is symmetric positive definite, and every updated diagonal block stays positive definite. `panel_blocks`: every entry lies within 8 / sqrt(128) of zero.
All inputs are finite; a program needn't handle non-finite values.
Results may differ from a plain program's by a relative error of at most 0.00095.
Values may be sent and summed in bfloat16 or wider, within the bound.
A program may use at most 64 MiB of HBM per device.

v0:
```python
import jax
import jax.numpy as jnp
from jax import lax
from jax.sharding import PartitionSpec as P


def spread(x, axis, root):
    mine = lax.axis_index(axis) == root
    return lax.psum(jnp.where(mine, x, jnp.zeros_like(x)), axis)


def from_partner(x, axis, apart):
    return lax.ppermute(x, axis, [(i, i ^ 1 << apart) for i in range(lax.axis_size(axis))])


def node_depth(parent, nodes):
    extended = jnp.concatenate([parent, jnp.array([nodes], jnp.int32)])
    depth = jnp.zeros((nodes,), jnp.int32)
    current = parent
    for index in range(nodes.bit_length()):
        depth = depth + (current < nodes).astype(jnp.int32)
        current = extended[current]
    return depth


def solve_right(lower, panel):

    def one(factor, block):
        return jax.scipy.linalg.solve_triangular(factor, block.T, lower=True).T

    return jax.vmap(one)(lower, panel)


def sibling_rank(target, nodes):
    earlier = jnp.arange(nodes)[None, :] < jnp.arange(nodes)[:, None]
    same = target[:, None] == target[None, :]
    return jnp.sum((same & earlier).astype(jnp.int32), axis=1)


def slot_picker(target, rank, active_nodes, owned_ids, count):
    match = target[None, None, :] == owned_ids[:, None, None]
    match = match & (rank[None, None, :] == jnp.arange(count)[None, :, None])
    match = match & active_nodes[None, None, :]
    return match.astype(jnp.bfloat16)


def select_rows(picker, block_list):
    return jnp.einsum("iqc,cab->iqab", picker, block_list, preferred_element_type=jnp.float32)


def outer_sum(block_list):
    return jnp.einsum("hync,hyxc->hnx", block_list, block_list, preferred_element_type=jnp.float32)


def cross_sum(left_factor, right_factor):
    return jnp.einsum(
        "hync,hyxc->hnx", left_factor, right_factor, preferred_element_type=jnp.float32
    )


def pair_cores(sent):
    return lax.all_gather(sent[:, None], "grp", axis=1, tiled=True)


def spread_nodes(sent, active_nodes, pick_near, pick_far, slots, nodes, present, blanks):
    paired = pair_cores(sent)
    order = jnp.argsort(jnp.where(active_nodes, 0, 1) * nodes + jnp.arange(nodes, dtype=jnp.int32))

    def visit(index, carry):
        node = order[index]
        piece = lax.dynamic_index_in_dim(paired, node % slots, 0, keepdims=False)
        arrived = spread(piece, "col", node // slots).astype(jnp.float32)
        weight_near = lax.dynamic_index_in_dim(pick_near, node, 2, keepdims=False).astype(
            jnp.float32
        )
        weight_far = lax.dynamic_index_in_dim(pick_far, node, 2, keepdims=False).astype(jnp.float32)
        return (
            carry[0] + weight_near[:, :, None, None] * arrived[0][None, None],
            carry[1] + weight_far[:, :, None, None] * arrived[1][None, None],
            carry[2] + weight_near[:, :, None, None] * arrived[1][None, None],
        )

    return lax.fori_loop(0, present, visit, blanks)


def shards(diag_blocks, panel_blocks, targets):
    slots = diag_blocks.shape[0]
    width = diag_blocks.shape[1]
    nodes = targets.shape[0]
    core = lax.axis_index("grp")
    owned_ids = lax.axis_index("col") * slots + jnp.arange(slots, dtype=jnp.int32)
    parent = targets[:, 0]
    grand = targets[:, 1]
    depth = node_depth(parent, nodes)
    rank_near = sibling_rank(parent, nodes)
    rank_far = sibling_rank(grand, nodes)
    owned_tree_depth = jnp.take(depth, owned_ids)
    acc_diag = diag_blocks
    acc_panel = panel_blocks[:, 0]
    out_diag = jnp.zeros_like(diag_blocks)
    output_panel = jnp.zeros_like(acc_panel)
    empty_pair_slots = jnp.zeros((slots, 2, width, width), jnp.float32)
    blank_four = jnp.zeros((slots, 4, width, width), jnp.float32)
    for level in range(nodes.bit_length() - 1, -1, -1):
        wide_mask = (owned_tree_depth == level)[:, None, None]
        lower = jnp.linalg.cholesky(acc_diag)
        solved = solve_right(lower, acc_panel)
        out_diag = jnp.where(wide_mask, lower, out_diag)
        output_panel = jnp.where(wide_mask, solved, output_panel)
        if level == 0:
            break
        sent = jnp.where(wide_mask, solved, 0.0).astype(jnp.bfloat16)
        active_nodes = depth == level
        pick_near = slot_picker(parent, rank_near, active_nodes, owned_ids, 2)
        pick_far = slot_picker(grand, rank_far, active_nodes, owned_ids, 4)
        present = min(2**level, nodes - 2**level + 1)
        crowded = present * 4 > nodes
        if crowded:
            piece = lax.all_gather(sent, "col", axis=0, tiled=True)
            near_rows = select_rows(pick_near, piece)
            far_rows = select_rows(pick_far, piece)
            near_rows = near_rows.astype(jnp.bfloat16)
            far_rows = far_rows.astype(jnp.bfloat16)
            own_update = lax.cond(
                core == 0, lambda: outer_sum(near_rows), lambda: outer_sum(far_rows)
            )
            other_update, other_rows = (
                from_partner(own_update.astype(jnp.bfloat16), "grp", 0).astype(own_update.dtype),
                from_partner(near_rows, "grp", 0),
            )
            schur_update = own_update + other_update
            cross = cross_sum(other_rows, near_rows)
        else:
            kids, grandkids, kids_far = spread_nodes(
                sent,
                active_nodes,
                pick_near,
                pick_far,
                slots,
                nodes,
                present,
                (empty_pair_slots, blank_four, empty_pair_slots),
            )
            kids = kids.astype(jnp.bfloat16)
            schur_update = outer_sum(kids) + outer_sum(grandkids.astype(jnp.bfloat16))
            cross = cross_sum(kids_far.astype(jnp.bfloat16), kids)
        acc_diag = acc_diag - schur_update
        acc_panel = acc_panel - jnp.where(core == 0, cross, 0.0)
    return (out_diag, output_panel[:, None])


def solution(mesh):
    placed = (P("col", None, None), P("col", "grp", None, None), P())
    return jax.shard_map(
        shards,
        mesh=mesh,
        in_specs=placed,
        out_specs=(P("col", None, None), P("col", "grp", None, None)),
        check_vma=False,
    )
```

profile of v0, /device:TPU:0, one launch (start us, length us, event | category | flops | bytes accessed | tf_op | source)
XLA Modules:
  0.0 962.0 jit_solution(17685611445959303273)
XLA Ops:
  7.9 0.7 gather_fusion
  8.6 0.7 gather_fusion.1
  9.3 0.7 gather_fusion.2
  10.0 0.7 gather_fusion.3
  10.7 0.7 dynamic-slice.2
  11.5 11.7 %custom-call.20 = f32[1,128,128]{2,1,0:T(8,128)S(1)} custom-call(f32[1,128,128]{2,1,0:T(8,128)S(1)} %fusion.50), custom_call_target="Cholesky" | custom-call | tf_op jit(solution)/shard_map/jit(cholesky)/cholesky | solution.py:106
  23.9 0.7 fusion.69
  24.5 9.8 %custom-call.21 = f32[1,1,128,128]{2,3,1,0:T(8,128)S(1)} custom-call(f32[1,1,128,128]{3,2,1,0:T(8,128)S(1)} %fusion.69), custom_call_target="InvertDiagBlocksLowerTriangular" | custom-call | tf_op jit(solution)/shard_map/vmap(jit(_solve_triangular))/triangular_solve | solution.py:29
  35.5 2.2 all-gather
  37.7 1.2 sort.45
  40.6 0.7 fusion.114
  41.4 0.7 fusion.112
  42.0 103.8 %all-reduce.4.cloned.1.call-done = bf16[2,128,128]{2,1,0:T(8,128)(2,1)} async-done(((bf16[2,128,128]{2,1,0:T(8,128)(2,1)}), bf16[2,128,128]{2,1,0:T(8,128)(2,1)}) %all-reduce.4.cloned.1.call-update) | async-done | bytes 65552 | tf_op jit(solution)/shard_map/while/body/eval_jaxpr/psum | solution.py:9
  145.9 0.8 convert_element_type.377
  147.6 11.7 %custom-call.22 = f32[1,128,128]{2,1,0:T(8,128)S(1)} custom-call(f32[1,128,128]{2,1,0:T(8,128)S(1)} %fusion.48), custom_call_target="Cholesky" | custom-call | tf_op jit(solution)/shard_map/jit(cholesky)/cholesky | solution.py:106
  159.3 0.7 compare_reduce_fusion.3
  160.7 9.8 %custom-call.23 = f32[1,1,128,128]{2,3,1,0:T(8,128)S(1)} custom-call(f32[1,1,128,128]{3,2,1,0:T(8,128)S(1)} %fusion.70), custom_call_target="InvertDiagBlocksLowerTriangular" | custom-call | tf_op jit(solution)/shard_map/vmap(jit(_solve_triangular))/triangular_solve | solution.py:29
  170.9 41.8 %all_gather.13 = bf16[16,128,128]{2,1,0:T(8,128)(2,1)S(1)} all-gather(bf16[1,128,128]{2,1,0:T(8,128)(2,1)S(1)} %copy.89), channel_id=1, replica_groups=mesh['col'=16,'grp'=2] {'col'}, dimensions={0}, use_global_device_ids=true | all-gather | bytes 557056 | tf_op jit(solution)/shard_map/all_gather | solution.py:119
  214.0 1.2 sort.46
  215.3 1.2 sort.47
  217.1 11.7 %custom-call.24 = f32[1,128,128]{2,1,0:T(8,128)S(1)} custom-call(f32[1,128,128]{2,1,0:T(8,128)S(1)} %fusion.45), custom_call_target="Cholesky" | custom-call | tf_op jit(solution)/shard_map/jit(cholesky)/cholesky | solution.py:106
  228.8 0.7 compare_reduce_fusion.2
  230.1 9.8 %custom-call.25 = f32[1,1,128,128]{2,3,1,0:T(8,128)S(1)} custom-call(f32[1,1,128,128]{3,2,1,0:T(8,128)S(1)} %fusion.71), custom_call_target="InvertDiagBlocksLowerTriangular" | custom-call | tf_op jit(solution)/shard_map/vmap(jit(_solve_triangular))/triangular_solve | solution.py:29
  240.6 2.1 all-gather.1
  242.7 438.1 %while.48 = (s32[]{:T(128)}, f32[1,2,128,128]{3,2,1,0:T(8,128)S(1)}, f32[1,4,128,128]{3,2,1,0:T(8,128)S(1)}, f32[1,2,128,128]{3,2,1,0:T(8,128)S(1)}, s32[16]{0:T...) while((s32[]{:T(128)}, ...), condition=%wide.region_11.14_spmd.clone, body=%wide.region_9.13_spmd.clone.sunk | while | flops 491536 | bytes 2228556 | solution.py:83
  242.7 0.7 dynamic_slice.120
  246.6 102.4 %all-reduce.6.cloned.1.call-done = bf16[2,128,128]{2,1,0:T(8,128)(2,1)} async-done(((bf16[2,128,128]{2,1,0:T(8,128)(2,1)}), bf16[2,128,128]{2,1,0:T(8,128)(2,1)}) %all-reduce.6.cloned.1.call-update) | async-done | bytes 65552 | tf_op jit(solution)/shard_map/while/body/eval_jaxpr/psum | solution.py:9
  349.0 0.8 convert_element_type.518
  350.1 0.7 dynamic_slice.120
  354.0 105.5 %all-reduce.6.cloned.1.call-done = bf16[2,128,128]{2,1,0:T(8,128)(2,1)} async-done(((bf16[2,128,128]{2,1,0:T(8,128)(2,1)}), bf16[2,128,128]{2,1,0:T(8,128)(2,1)}) %all-reduce.6.cloned.1.call-update) | async-done | bytes 65552 | tf_op jit(solution)/shard_map/while/body/eval_jaxpr/psum | solution.py:9
  459.4 0.8 convert_element_type.518
  464.4 105.2 %all-reduce.6.cloned.1.call-done = bf16[2,128,128]{2,1,0:T(8,128)(2,1)} async-done(((bf16[2,128,128]{2,1,0:T(8,128)(2,1)}), bf16[2,128,128]{2,1,0:T(8,128)(2,1)}) %all-reduce.6.cloned.1.call-update) | async-done | bytes 65552 | tf_op jit(solution)/shard_map/while/body/eval_jaxpr/psum | solution.py:9
  569.6 0.8 convert_element_type.518
  574.5 105.2 %all-reduce.6.cloned.1.call-done = bf16[2,128,128]{2,1,0:T(8,128)(2,1)} async-done(((bf16[2,128,128]{2,1,0:T(8,128)(2,1)}), bf16[2,128,128]{2,1,0:T(8,128)(2,1)}) %all-reduce.6.cloned.1.call-update) | async-done | bytes 65552 | tf_op jit(solution)/shard_map/while/body/eval_jaxpr/psum | solution.py:9
  679.7 0.8 convert_element_type.518
  681.3 11.7 %custom-call.26 = f32[1,128,128]{2,1,0:T(8,128)S(1)} custom-call(f32[1,128,128]{2,1,0:T(8,128)S(1)} %fusion.41), custom_call_target="Cholesky" | custom-call | tf_op jit(solution)/shard_map/jit(cholesky)/cholesky | solution.py:106
  693.0 0.7 compare_reduce_fusion.1
  694.4 9.8 %custom-call.27 = f32[1,1,128,128]{2,3,1,0:T(8,128)S(1)} custom-call(f32[1,1,128,128]{3,2,1,0:T(8,128)S(1)} %fusion.72), custom_call_target="InvertDiagBlocksLowerTriangular" | custom-call | tf_op jit(solution)/shard_map/vmap(jit(_solve_triangular))/triangular_solve | solution.py:29
  704.8 2.2 all-gather.2
  706.9 220.6 %while.49 = (s32[]{:T(128)}, f32[1,2,128,128]{3,2,1,0:T(8,128)S(1)}, f32[1,4,128,128]{3,2,1,0:T(8,128)S(1)}, f32[1,2,128,128]{3,2,1,0:T(8,128)S(1)}, s32[16]{0:T...) while((s32[]{:T(128)}, ...), condition=%wide.region_15.18_spmd.clone, body=%wide.region_13.17_spmd.clone.sunk | while | flops 491536 | bytes 2228556 | solution.py:83
  710.8 105.1 %all-reduce.8.cloned.1.call-done = bf16[2,128,128]{2,1,0:T(8,128)(2,1)} async-done(((bf16[2,128,128]{2,1,0:T(8,128)(2,1)}), bf16[2,128,128]{2,1,0:T(8,128)(2,1)}) %all-reduce.8.cloned.1.call-update) | async-done | bytes 65552 | tf_op jit(solution)/shard_map/while/body/eval_jaxpr/psum | solution.py:9
  816.0 0.8 convert_element_type.519
  821.0 105.4 %all-reduce.8.cloned.1.call-done = bf16[2,128,128]{2,1,0:T(8,128)(2,1)} async-done(((bf16[2,128,128]{2,1,0:T(8,128)(2,1)}), bf16[2,128,128]{2,1,0:T(8,128)(2,1)}) %all-reduce.8.cloned.1.call-update) | async-done | bytes 65552 | tf_op jit(solution)/shard_map/while/body/eval_jaxpr/psum | solution.py:9
  926.4 0.8 convert_element_type.519
  928.0 11.7 %custom-call.28 = f32[1,128,128]{2,1,0:T(8,128)S(1)} custom-call(f32[1,128,128]{2,1,0:T(8,128)S(1)} %fusion.36), custom_call_target="Cholesky" | custom-call | tf_op jit(solution)/shard_map/jit(cholesky)/cholesky | solution.py:106
  940.4 3.8 select_bitcast_fusion.2
  944.2 9.8 %custom-call.29 = f32[1,1,128,128]{2,3,1,0:T(8,128)S(1)} custom-call(f32[1,1,128,128]{3,2,1,0:T(8,128)S(1)} %get-tuple-element.605), custom_call_target="InvertDiagBlocksLowerTriangular" | custom-call | tf_op jit(solution)/shard_map/vmap(jit(_solve_triangular))/triangular_solve | solution.py:29
  954.5 0.7 copy.107
  (140 shorter events, 19.9 us)
Async XLA Ops:
  7.2 0.7 copy-start.2
  7.2 138.7 %all-reduce.4.cloned.1.call-start = ((), (), s32[]{:S(2)}) async-start(), calls=%async_computation | async-start | bytes 131072 | tf_op jit(solution)/shard_map/while/body/eval_jaxpr/psum | solution.py:9
  10.0 1.4 copy-start
  23.9 11.2 %copy-start.1 = (f32[1,1,128,128]{3,2,1,0:T(8,128)S(1)}, f32[1,1,128,128]{3,2,1,0:T(8,128)}, u32[]{:S(2)}) copy-start(f32[1,1,128,128]{3,2,1,0:T(8,128)} %param.14) | copy-start | bytes 196612
  213.9 3.1 collective-permute-start
  216.5 23.4 %collective-permute-start.1 = (bf16[1,2,128,128]{3,1,2,0:T(2,128)(2,1)S(1)}, bf16[1,2,128,128]{3,1,2,0:T(2,128)(2,1)S(1)}, u32[]{:S(2)}, u32[]{:S(2)}) collective-permute-start(bf16[1,2,128,128]{3,1,2,0:T(2,128)(2,1)S(1)} %bitcast.322), channel_id=1, source_target_pairs={{0,1},{1,0},{2,3},{3,2},{4,5},{5,4},{6,7},{7,6},{8,9},{9,8},{10,11... | collective-permute-start | bytes 196616 | tf_op jit(solution)/shard_map/ppermute | solution.py:13
  242.7 106.3 %all-reduce.6.cloned.1.call-start = ((), (), s32[]{:S(2)}) async-start(), calls=%async_computation.1 | async-start | bytes 131072 | tf_op jit(solution)/shard_map/while/body/eval_jaxpr/psum | solution.py:9
  350.0 109.4 %all-reduce.6.cloned.1.call-start = ((), (), s32[]{:S(2)}) async-start(), calls=%async_computation.1 | async-start | bytes 131072 | tf_op jit(solution)/shard_map/while/body/eval_jaxpr/psum | solution.py:9
  460.5 109.1 %all-reduce.6.cloned.1.call-start = ((), (), s32[]{:S(2)}) async-start(), calls=%async_computation.1 | async-start | bytes 131072 | tf_op jit(solution)/shard_map/while/body/eval_jaxpr/psum | solution.py:9
  570.6 109.1 %all-reduce.6.cloned.1.call-start = ((), (), s32[]{:S(2)}) async-start(), calls=%async_computation.1 | async-start | bytes 131072 | tf_op jit(solution)/shard_map/while/body/eval_jaxpr/psum | solution.py:9
  706.9 109.0 %all-reduce.8.cloned.1.call-start = ((), (), s32[]{:S(2)}) async-start(), calls=%async_computation.2 | async-start | bytes 131072 | tf_op jit(solution)/shard_map/while/body/eval_jaxpr/psum | solution.py:9
  817.1 109.4 %all-reduce.8.cloned.1.call-start = ((), (), s32[]{:S(2)}) async-start(), calls=%async_computation.2 | async-start | bytes 131072 | tf_op jit(solution)/shard_map/while/body/eval_jaxpr/psum | solution.py:9
Sparse Core Ops, SparseCore 0:
  39.7 106.0 all-reduce.3
  249.5 99.3 all-reduce.5
  356.9 102.4 all-reduce.5
  467.0 102.4 all-reduce.5
  577.2 102.4 all-reduce.5
  713.5 102.4 all-reduce.7
  823.9 102.4 all-reduce.7
where the time goes:
time: 963 us; the launch traced here: 962 us
  waiting for transfers between devices  733 us (76%)
  other arithmetic  135 us (14%)
  blocking collectives  48.3 us (5%)
  loops' own time  15.8 us (2%)
  between operations  15.4 us (2%)
  local copies, waits for them, and re-layouts  10 us (1%)
    psum x7, waiting for transfers between devices, spread(): return lax.psum(jnp.where(mine, x, jnp.zeros_like(x)), axis)  733 us
    another operation x15, other arithmetic, shards(): lower = jnp.linalg.cholesky(acc_diag)  62.1 us
    another operation x10, other arithmetic, one(): return jax.scipy.linalg.solve_triangular(factor, block.T, lower=True).T  55.4 us
    all_gather x1, blocking collectives, shards(): piece = lax.all_gather(sent, 'col', axis=0, tiled=True)  41.8 us
  transfers between devices with their start and end apart: 9, of which 7 were waited for; matrix products, arithmetic and copies ran while one was open for 3% of the time, Pallas kernels for 0%

commit v1 on v0

--- a/solution.py
+++ b/solution.py
@@ -6,7 +6,7 @@
 
 def spread(x, axis, root):
     mine = lax.axis_index(axis) == root
-    return lax.psum(jnp.where(mine, x, jnp.zeros_like(x)), axis)
+    return jnp.sum(lax.all_gather(jnp.where(mine, x, jnp.zeros_like(x)), axis), axis=0)
 
 
 def from_partner(x, axis, apart):

time: 963 us -> 611 us (0.63)
  waiting for transfers between devices: 733 us -> 377 us
    psum x7 -> x0, waiting for transfers between devices: 733 us -> none  [spread(): return lax.psum(jnp.where(mine, x, jnp.zeros_like(x)), axis)]
    all_gather x0 -> x7, waiting for transfers between devices: none -> 377 us  [spread(): lax.all_gather(jnp.where(mine, x, jnp.zeros_like(x)), axis)]
  transfers between devices with their start and end apart: 9 -> 9, of which waited for: 7 -> 7; matrix products, arithmetic and copies ran while one was open for 3% -> 5% of each run, Pallas kernels for 0% -> 0%
where the time goes in v1:
time: 611 us; the launch traced here: 610 us
  waiting for transfers between devices  377 us (62%)
  other arithmetic  139 us (23%)
  blocking collectives  47.9 us (8%)
  loops' own time  15.8 us (3%)
  between operations  15.5 us (3%)
  local copies, waits for them, and re-layouts  10.3 us (2%)
    all_gather x7, waiting for transfers between devices, spread(): lax.all_gather(jnp.where(mine, x, jnp.zeros_like(x)), axis)  377 us
    another operation x15, other arithmetic, shards(): lower = jnp.linalg.cholesky(acc_diag)  62.1 us
    another operation x10, other arithmetic, one(): return jax.scipy.linalg.solve_triangular(factor, block.T, lower=True).T  55.3 us
    all_gather x1, blocking collectives, shards(): piece = lax.all_gather(sent, 'col', axis=0, tiled=True)  41.5 us
    another operation x2, loops' own time, spread_nodes(): return lax.fori_loop(0, present, visit, blanks)  15.6 us
  transfers between devices with their start and end apart: 9, of which 7 were waited for; matrix products, arithmetic and copies ran while one was open for 5% of the time, Pallas kernels for 0%

profile of v1, /device:TPU:0, one launch (start us, length us, event | category | flops | bytes accessed | tf_op | source)
XLA Modules:
  0.0 609.9 jit_solution(17946104404329501114)
XLA Ops:
  7.9 0.7 gather_fusion
  8.6 0.7 gather_fusion.1
  9.3 0.7 gather_fusion.2
  10.0 0.7 gather_fusion.3
  10.7 0.7 dynamic-slice.2
  11.5 11.7 %custom-call.20 = f32[1,128,128]{2,1,0:T(8,128)S(1)} custom-call(f32[1,128,128]{2,1,0:T(8,128)S(1)} %fusion.50), custom_call_target="Cholesky" | custom-call | tf_op jit(solution)/shard_map/jit(cholesky)/cholesky | solution.py:106
  24.5 9.8 %custom-call.21 = f32[1,1,128,128]{2,3,1,0:T(8,128)S(1)} custom-call(f32[1,1,128,128]{3,2,1,0:T(8,128)S(1)} %fusion.69), custom_call_target="InvertDiagBlocksLowerTriangular" | custom-call | tf_op jit(solution)/shard_map/vmap(jit(_solve_triangular))/triangular_solve | solution.py:29
  35.4 2.2 all-gather
  37.6 1.2 sort.45
  40.5 0.7 fusion.114
  41.3 0.7 fusion.112
  42.0 55.4 %all-gather.8.cloned.1.call-done = bf16[32,128,128]{2,1,0:T(8,128)(2,1)} async-done(((bf16[2,128,128]{2,1,0:T(8,128)(2,1)}), bf16[32,128,128]{2,1,0:T(8,128)(2,1)}) %all-gather.8.cloned.1.call-update) | async-done | bytes 1048592 | tf_op jit(solution)/shard_map/while/body/eval_jaxpr/all_gather | solution.py:9
  97.4 1.4 reduce_sum.60
  100.0 11.7 %custom-call.22 = f32[1,128,128]{2,1,0:T(8,128)S(1)} custom-call(f32[1,128,128]{2,1,0:T(8,128)S(1)} %fusion.48), custom_call_target="Cholesky" | custom-call | tf_op jit(solution)/shard_map/jit(cholesky)/cholesky | solution.py:106
  111.7 0.7 compare_reduce_fusion.3
  113.1 9.8 %custom-call.23 = f32[1,1,128,128]{2,3,1,0:T(8,128)S(1)} custom-call(f32[1,1,128,128]{3,2,1,0:T(8,128)S(1)} %fusion.70), custom_call_target="InvertDiagBlocksLowerTriangular" | custom-call | tf_op jit(solution)/shard_map/vmap(jit(_solve_triangular))/triangular_solve | solution.py:29
  123.3 41.5 %all_gather.46 = bf16[16,128,128]{2,1,0:T(8,128)(2,1)S(1)} all-gather(bf16[1,128,128]{2,1,0:T(8,128)(2,1)S(1)} %copy.91), channel_id=1, replica_groups=mesh['col'=16,'grp'=2] {'col'}, dimensions={0}, use_global_device_ids=true | all-gather | bytes 557056 | tf_op jit(solution)/shard_map/all_gather | solution.py:119
  166.1 1.2 sort.46
  167.4 1.2 sort.47
  169.2 11.7 %custom-call.24 = f32[1,128,128]{2,1,0:T(8,128)S(1)} custom-call(f32[1,128,128]{2,1,0:T(8,128)S(1)} %fusion.45), custom_call_target="Cholesky" | custom-call | tf_op jit(solution)/shard_map/jit(cholesky)/cholesky | solution.py:106
  180.9 0.7 compare_reduce_fusion.2
  182.2 9.8 %custom-call.25 = f32[1,1,128,128]{2,3,1,0:T(8,128)S(1)} custom-call(f32[1,1,128,128]{3,2,1,0:T(8,128)S(1)} %fusion.71), custom_call_target="InvertDiagBlocksLowerTriangular" | custom-call | tf_op jit(solution)/shard_map/vmap(jit(_solve_triangular))/triangular_solve | solution.py:29
  192.7 2.1 all-gather.1
  194.8 235.4 %while.48 = (s32[]{:T(128)}, f32[1,2,128,128]{3,2,1,0:T(8,128)S(1)}, f32[1,4,128,128]{3,2,1,0:T(8,128)S(1)}, f32[1,2,128,128]{3,2,1,0:T(8,128)S(1)}, s32[16]{0:T...) while((s32[]{:T(128)}, ...), condition=%wide.region_11.14_spmd.clone, body=%wide.region_9.13_spmd.clone.sunk | while | flops 950288 | bytes 6291798 | solution.py:83
  194.8 0.7 dynamic_slice.120
  198.7 51.3 %all-gather.10.cloned.1.call-done = bf16[16,2,128,128]{3,2,1,0:T(8,128)(2,1)} async-done(((bf16[1,2,128,128]{3,2,1,0:T(8,128)(2,1)}), bf16[16,2,128,128]{3,2,1,0:T(8,128)(2,1)}) %all-gather.10.cloned.1.call-update) | async-done | bytes 1048592 | tf_op jit(solution)/shard_map/while/body/eval_jaxpr/all_gather | solution.py:9
  250.0 1.4 reduce_sum.68
  251.6 0.7 dynamic_slice.120
  255.5 54.2 %all-gather.10.cloned.1.call-done = bf16[16,2,128,128]{3,2,1,0:T(8,128)(2,1)} async-done(((bf16[1,2,128,128]{3,2,1,0:T(8,128)(2,1)}), bf16[16,2,128,128]{3,2,1,0:T(8,128)(2,1)}) %all-gather.10.cloned.1.call-update) | async-done | bytes 1048592 | tf_op jit(solution)/shard_map/while/body/eval_jaxpr/all_gather | solution.py:9
  309.7 1.4 reduce_sum.68
  311.4 0.7 dynamic_slice.120
  315.2 53.9 %all-gather.10.cloned.1.call-done = bf16[16,2,128,128]{3,2,1,0:T(8,128)(2,1)} async-done(((bf16[1,2,128,128]{3,2,1,0:T(8,128)(2,1)}), bf16[16,2,128,128]{3,2,1,0:T(8,128)(2,1)}) %all-gather.10.cloned.1.call-update) | async-done | bytes 1048592 | tf_op jit(solution)/shard_map/while/body/eval_jaxpr/all_gather | solution.py:9
  369.1 1.4 reduce_sum.68
  374.6 53.9 %all-gather.10.cloned.1.call-done = bf16[16,2,128,128]{3,2,1,0:T(8,128)(2,1)} async-done(((bf16[1,2,128,128]{3,2,1,0:T(8,128)(2,1)}), bf16[16,2,128,128]{3,2,1,0:T(8,128)(2,1)}) %all-gather.10.cloned.1.call-update) | async-done | bytes 1048592 | tf_op jit(solution)/shard_map/while/body/eval_jaxpr/all_gather | solution.py:9
  428.5 1.4 reduce_sum.68
  430.6 11.7 %custom-call.26 = f32[1,128,128]{2,1,0:T(8,128)S(1)} custom-call(f32[1,128,128]{2,1,0:T(8,128)S(1)} %fusion.41), custom_call_target="Cholesky" | custom-call | tf_op jit(solution)/shard_map/jit(cholesky)/cholesky | solution.py:106
  442.4 0.7 compare_reduce_fusion.1
  443.7 9.8 %custom-call.27 = f32[1,1,128,128]{2,3,1,0:T(8,128)S(1)} custom-call(f32[1,1,128,128]{3,2,1,0:T(8,128)S(1)} %fusion.72), custom_call_target="InvertDiagBlocksLowerTriangular" | custom-call | tf_op jit(solution)/shard_map/vmap(jit(_solve_triangular))/triangular_solve | solution.py:29
  454.1 2.2 all-gather.2
  456.3 119.1 %while.49 = (s32[]{:T(128)}, f32[1,2,128,128]{3,2,1,0:T(8,128)S(1)}, f32[1,4,128,128]{3,2,1,0:T(8,128)S(1)}, f32[1,2,128,128]{3,2,1,0:T(8,128)S(1)}, s32[16]{0:T...) while((s32[]{:T(128)}, ...), condition=%wide.region_15.18_spmd.clone, body=%wide.region_13.17_spmd.clone.sunk | while | flops 950288 | bytes 6291798 | solution.py:83
  460.2 53.9 %all-gather.12.cloned.1.call-done = bf16[16,2,128,128]{3,2,1,0:T(8,128)(2,1)} async-done(((bf16[1,2,128,128]{3,2,1,0:T(8,128)(2,1)}), bf16[16,2,128,128]{3,2,1,0:T(8,128)(2,1)}) %all-gather.12.cloned.1.call-update) | async-done | bytes 1048592 | tf_op jit(solution)/shard_map/while/body/eval_jaxpr/all_gather | solution.py:9
  514.1 1.4 reduce_sum.69
  519.6 54.2 %all-gather.12.cloned.1.call-done = bf16[16,2,128,128]{3,2,1,0:T(8,128)(2,1)} async-done(((bf16[1,2,128,128]{3,2,1,0:T(8,128)(2,1)}), bf16[16,2,128,128]{3,2,1,0:T(8,128)(2,1)}) %all-gather.12.cloned.1.call-update) | async-done | bytes 1048592 | tf_op jit(solution)/shard_map/while/body/eval_jaxpr/all_gather | solution.py:9
  573.8 1.4 reduce_sum.69
  575.9 11.7 %custom-call.28 = f32[1,128,128]{2,1,0:T(8,128)S(1)} custom-call(f32[1,128,128]{2,1,0:T(8,128)S(1)} %fusion.36), custom_call_target="Cholesky" | custom-call | tf_op jit(solution)/shard_map/jit(cholesky)/cholesky | solution.py:106
  588.3 3.7 select_bitcast_fusion
  592.0 9.8 %custom-call.29 = f32[1,1,128,128]{2,3,1,0:T(8,128)S(1)} custom-call(f32[1,1,128,128]{3,2,1,0:T(8,128)S(1)} %get-tuple-element.607), custom_call_target="InvertDiagBlocksLowerTriangular" | custom-call | tf_op jit(solution)/shard_map/vmap(jit(_solve_triangular))/triangular_solve | solution.py:29
  602.3 0.7 copy.109
  (150 shorter events, 20.2 us)
Async XLA Ops:
  7.2 0.7 copy-start.2
  7.2 90.2 %all-gather.8.cloned.1.call-start = ((), (), s32[]{:S(2)}) async-start(), calls=%async_computation | async-start | bytes 1114112 | tf_op jit(solution)/shard_map/while/body/eval_jaxpr/all_gather | solution.py:9
  10.0 1.4 copy-start
  23.9 11.1 %copy-start.1 = (f32[1,1,128,128]{3,2,1,0:T(8,128)S(1)}, f32[1,1,128,128]{3,2,1,0:T(8,128)}, u32[]{:S(2)}) copy-start(f32[1,1,128,128]{3,2,1,0:T(8,128)} %param.14) | copy-start | bytes 196612
  166.0 3.1 collective-permute-start
  168.6 23.4 %collective-permute-start.1 = (bf16[1,2,128,128]{3,1,2,0:T(2,128)(2,1)S(1)}, bf16[1,2,128,128]{3,1,2,0:T(2,128)(2,1)S(1)}, u32[]{:S(2)}, u32[]{:S(2)}) collective-permute-start(bf16[1,2,128,128]{3,1,2,0:T(2,128)(2,1)S(1)} %bitcast.316), channel_id=1, source_target_pairs={{0,1},{1,0},{2,3},{3,2},{4,5},{5,4},{6,7},{7,6},{8,9},{9,8},{10,11... | collective-permute-start | bytes 196616 | tf_op jit(solution)/shard_map/ppermute | solution.py:13
  194.8 55.2 %all-gather.10.cloned.1.call-start = ((), (), s32[]{:S(2)}) async-start(), calls=%async_computation.1 | async-start | bytes 1114112 | tf_op jit(solution)/shard_map/while/body/eval_jaxpr/all_gather | solution.py:9
  251.6 58.1 %all-gather.10.cloned.1.call-start = ((), (), s32[]{:S(2)}) async-start(), calls=%async_computation.1 | async-start | bytes 1114112 | tf_op jit(solution)/shard_map/while/body/eval_jaxpr/all_gather | solution.py:9
  311.3 57.8 %all-gather.10.cloned.1.call-start = ((), (), s32[]{:S(2)}) async-start(), calls=%async_computation.1 | async-start | bytes 1114112 | tf_op jit(solution)/shard_map/while/body/eval_jaxpr/all_gather | solution.py:9
  370.7 57.8 %all-gather.10.cloned.1.call-start = ((), (), s32[]{:S(2)}) async-start(), calls=%async_computation.1 | async-start | bytes 1114112 | tf_op jit(solution)/shard_map/while/body/eval_jaxpr/all_gather | solution.py:9
  456.3 57.8 %all-gather.12.cloned.1.call-start = ((), (), s32[]{:S(2)}) async-start(), calls=%async_computation.2 | async-start | bytes 1114112 | tf_op jit(solution)/shard_map/while/body/eval_jaxpr/all_gather | solution.py:9
  515.7 58.1 %all-gather.12.cloned.1.call-start = ((), (), s32[]{:S(2)}) async-start(), calls=%async_computation.2 | async-start | bytes 1114112 | tf_op jit(solution)/shard_map/while/body/eval_jaxpr/all_gather | solution.py:9
Sparse Core Ops, SparseCore 0:
  39.7 57.6 all-gather.7
  198.9 50.9 all-gather.9
  255.7 53.9 all-gather.9
  315.2 53.9 all-gather.9
  374.6 53.9 all-gather.9
  460.1 53.9 all-gather.11
  519.8 53.9 all-gather.11
